TPU v7x, 128 devices: a whole 4x4x4 slice. The times are simulated.
128 devices in a mesh: clip: 2 (over core), tm: 16 (over z, x), head: 4 (over y).
Axes of the slice: x: 4, y: 4, z: 4, core: 2. Of those that a mesh axis runs over, the one named last changes fastest.
Arguments:
- video_tokens: bfloat16 [64, 1568, 1024], P(('clip', 'tm')), parts along dimension 0, may hold values from -6 to 6
- window_order: int32 [64, 1568], P(('clip', 'tm')), parts along dimension 0, may hold values from 0 to 1567, each once within a row
- clip_id: int32 [64], P(('clip', 'tm')), parts along dimension 0, may hold values from 0 to 7, never falling along the last dimension, each value on 1 to 8 neighbouring positions
- attend_weight: bfloat16 [3, 1024, 1024], P(None, None, 'head'), may hold values from -0.75 to 0.75
- attend_out: bfloat16 [1024, 1024], P('head'), may hold values from -0.1875 to 0.1875
- recur_weight: bfloat16 [3, 1024, 1024], P(None, None, 'head'), may hold values from -0.1875 to 0.1875
- frame_decay: float32 [64, 1024], P(('clip', 'tm'), 'head'), parts along dimension 0, may hold values from -5.7 to -0.010625, as said below
- recur_out: bfloat16 [1024, 1024], P('head'), may hold values from -0.1875 to 0.1875
Outputs:
- features_out: bfloat16 [64, 1568, 1024], P(('clip', 'tm'), None, 'head'), parts along dimension 0
There are 2 independent parts, one for each index of `clip`. A program takes and returns all parts, laid end to end along the dimension named above; an argument that names none is the same for every part. Nothing has to cross between parts.
Inputs may be any that keep to these rules, and one draw needn't show every extreme that they name: `clip_id`: never falls along the frames; a clip spans 1 to 8 frames. `frame_decay`: negative.
All inputs are finite; a program needn't handle non-finite values.
Results may differ from a plain program's by a relative error of at most 0.01.
Values may be sent and summed in bfloat16 or wider, within the bound.
No kernel may reach another device: no remote copies, remote signals or barrier semaphores. Data moves between devices by JAX's collectives and lax.ppermute only.
A program may use at most 128 MiB of HBM per device.

v0:
```python
import jax
import jax.numpy as jnp
from jax import lax
from jax.sharding import PartitionSpec as P

HEAD_DIMENSION = 64
WINDOW = 49
EPSILON = 1e-06


def from_behind(value, axis, steps):
    count = lax.axis_size(axis)
    leading, last = (max(0, -steps), min(count, count - steps))
    return lax.ppermute(value, axis, [(source, source + steps) for source in range(leading, last)])


def normalize(values):
    return values * lax.rsqrt(jnp.mean(values * values, axis=-1, keepdims=True) + EPSILON)


def window_attention(queries, keys_all, values_all, window_order):
    frame_count, positions, number_of_heads, head_size = queries.shape
    order_index = window_order[:, :, None, None]

    def arrange(tensor):
        reordered = jnp.take_along_axis(tensor, order_index, axis=1)
        return reordered.reshape(
            frame_count, positions // WINDOW, WINDOW, number_of_heads, head_size
        )

    scores = jnp.einsum(
        "fwihe,fwjhe->fwhij",
        arrange(queries),
        arrange(keys_all),
        preferred_element_type=jnp.float32,
    ) / jnp.sqrt(jnp.float32(head_size))
    weights = jax.nn.softmax(scores, axis=-1).astype(jnp.bfloat16)
    blended = jnp.einsum(
        "fwhij,fwjhe->fwihe", weights, arrange(values_all), preferred_element_type=jnp.float32
    ).astype(jnp.bfloat16)
    blended = blended.reshape(frame_count, positions, number_of_heads, head_size)
    inverse = jnp.argsort(window_order, axis=1)
    return jnp.take_along_axis(blended, inverse[:, :, None, None], axis=1)


def per_device(
    video_tokens,
    window_order,
    clip_id,
    attend_weight,
    attend_out,
    recur_weight,
    frame_decay,
    recur_out,
):
    frame_count, positions, model_width = video_tokens.shape
    local_width = attend_weight.shape[2]
    row_count = frame_count * positions
    inputs = video_tokens.reshape(row_count, model_width).astype(jnp.float32)
    normed = normalize(inputs).astype(jnp.bfloat16)
    projected = jnp.einsum(
        "td,kde->kte", normed, attend_weight, preferred_element_type=jnp.float32
    ).astype(jnp.bfloat16)
    shaped = projected.reshape(
        3, frame_count, positions, local_width // HEAD_DIMENSION, HEAD_DIMENSION
    )
    attended = window_attention(shaped[0], shaped[1], shaped[2], window_order).reshape(
        row_count, local_width
    )
    partial_mix = jnp.dot(attended, attend_out, preferred_element_type=jnp.float32)
    offset = lax.axis_index("head") * local_width
    residual = inputs + lax.psum(partial_mix.astype(jnp.bfloat16), "head").astype(jnp.float32)
    normed_again = normalize(residual).astype(jnp.bfloat16)
    recur_proj = jnp.einsum(
        "td,kde->kte", normed_again, recur_weight, preferred_element_type=jnp.float32
    )
    residual_own = lax.dynamic_slice_in_dim(residual, offset, local_width, 1)
    gate_in = jax.nn.sigmoid(recur_proj[0]).reshape(frame_count, positions, local_width)
    value_in = recur_proj[1].reshape(frame_count, positions, local_width)
    out_gate = jax.nn.silu(recur_proj[2]).reshape(frame_count, positions, local_width)
    retain = jnp.exp(frame_decay)
    driven = jnp.sqrt(1.0 - retain * retain)[:, None, :] * gate_in * value_in
    previous = from_behind(clip_id[frame_count - 1 :], "tm", 1)
    continues = jnp.concatenate(
        [
            (clip_id[:1] == previous).astype(jnp.float32),
            (clip_id[1:] == clip_id[:-1]).astype(jnp.float32),
        ]
    )
    factor = retain * continues[:, None]

    def advance(carried, inputs_now):
        decay_total, state_now = carried
        factor_now, driven_now = inputs_now
        decay_total = factor_now * decay_total
        state_now = factor_now[None, :] * state_now + driven_now
        return ((decay_total, state_now), (decay_total, state_now))

    start_carry = (
        jnp.ones((local_width,), jnp.float32),
        jnp.zeros((positions, local_width), jnp.float32),
    )
    last_carry, all_carry = lax.scan(advance, start_carry, (factor, driven))
    decay_last, state_last = last_carry
    decay_all, state_all = all_carry

    def relay_step(counter, incoming):
        outgoing = decay_last[None, :] * incoming + state_last
        return from_behind(outgoing.astype(jnp.bfloat16), "tm", 1).astype(outgoing.dtype)

    incoming = lax.fori_loop(
        0, lax.axis_size("tm") - 1, relay_step, jnp.zeros((positions, local_width), jnp.float32)
    )
    states = state_all + decay_all[:, None, :] * incoming[None, :, :]
    output_rows = (states * out_gate).astype(jnp.bfloat16).reshape(row_count, local_width)
    partial_out = jnp.dot(output_rows, recur_out, preferred_element_type=jnp.float32)
    result = residual_own + lax.psum_scatter(
        partial_out.astype(jnp.bfloat16), "head", scatter_dimension=1, tiled=True
    ).astype(jnp.float32)
    return result.astype(jnp.bfloat16).reshape(frame_count, positions, local_width)


def solution(mesh):
    return jax.shard_map(
        per_device,
        mesh=mesh,
        in_specs=(
            P(("clip", "tm"), None, None),
            P(("clip", "tm"), None),
            P(("clip", "tm")),
            P(None, None, "head"),
            P("head", None),
            P(None, None, "head"),
            P(("clip", "tm"), "head"),
            P("head", None),
        ),
        out_specs=P(("clip", "tm"), None, "head"),
        check_vma=False,
    )
```

profile of v0, /device:TPU:1, one launch (start us, length us, event | category | flops | bytes accessed | tf_op | source)
XLA Modules:
  0.0 906.6 jit_solution(7665723979493977932)
XLA Ops:
  33.3 28.2 %gather_fusion = bf16[3136,4,64]{2,1,0:T(4,128)(2,1)} fusion(bf16[2,1568,4,64]{3,2,1,0:T(4,128)(2,1)} %reshape.168, s32[3136]{0:T(1024)S(1)} %reshape.147), kind=kCustom, calls=%fused_computation.clone | custom fusion | bytes 3236352 | tf_op jit(solution)/shard_map/jit(take_along_axis)/gather | solution.py:26
  75.9 37.3 %gather_fusion.1 = bf16[3136,4,64]{2,1,0:T(4,128)(2,1)} fusion(bf16[2,1568,4,64]{3,2,1,0:T(4,128)(2,1)} %reshape.170, s32[3136]{0:T(1024)S(1)} %reshape.147), kind=kCustom, calls=%fused_computation.1.clone | custom fusion | bytes 3236352 | tf_op jit(solution)/shard_map/jit(take_along_axis)/gather | solution.py:26
  113.2 9.4 %copy.43 = bf16[2,1568,4,64]{1,0,3,2:T(2,128)(2,1)} copy(bf16[2,1568,4,64]{3,2,1,0:T(4,128)(2,1)} %bitcast.90) | data formatting | bytes 3211264 | tf_op jit(solution)/shard_map/jit(take_along_axis)/gather | solution.py:26
  128.5 28.5 %gather_fusion.2 = bf16[3136,4,64]{2,1,0:T(4,128)(2,1)} fusion(bf16[2,1568,4,64]{3,2,1,0:T(4,128)(2,1)} %reshape.172, s32[3136]{0:T(1024)S(1)} %reshape.147), kind=kCustom, calls=%fused_computation.2.clone | custom fusion | bytes 3236352 | tf_op jit(solution)/shard_map/jit(take_along_axis)/gather | solution.py:26
  173.3 15.7 %reshape.171 = bf16[2,32,49,4,64]{2,1,0,4,3:T(8,128)(2,1)} reshape(bf16[2,1568,4,64]{1,0,3,2:T(2,128)(2,1)} %get-tuple-element.145) | data formatting | bytes 3211264 | tf_op jit(solution)/shard_map/reshape | solution.py:27
  189.0 14.4 %reshape.173 = bf16[2,32,49,4,64]{2,1,0,4,3:T(8,128)(2,1)} reshape(bf16[2,1568,4,64]{1,0,3,2:T(2,128)(2,1)S(1)} %copy-done.3) | data formatting | bytes 3211264 | tf_op jit(solution)/shard_map/reshape | solution.py:27
  203.3 15.2 %fusion.15 = f32[2,32,4,49,49]{3,4,2,1,0:T(8,128)S(1)} fusion(bf16[2,32,49,4,64]{2,1,0,4,3:T(8,128)(2,1)} %reshape.173, bf16[2,32,49,4,64]{2,1,0,4,3:T(8,128)(2,1)} %reshape.171), kind=kOutput, calls=%fused_computation.32 | convolution fusion | flops 78675968 | bytes 5669888 | tf_op jit(solution)/shard_map/fwihe,fwjhe->fwhij/dot_general | solution.py:31
  224.1 14.4 %reshape.169 = bf16[2,32,49,4,64]{2,1,0,4,3:T(8,128)(2,1)} reshape(bf16[2,1568,4,64]{1,0,3,2:T(2,128)(2,1)S(1)} %copy-done.2) | data formatting | bytes 3211264 | tf_op jit(solution)/shard_map/reshape | solution.py:27
  238.5 13.6 %convert_bitcast_fusion = bf16[2,32,49,4,64]{4,2,3,1,0:T(8,128)(2,1)S(1)} fusion(f32[2,32,4,49,49]{3,4,2,1,0:T(8,128)} %get-tuple-element.152, f32[2,32,4,49]{3,2,1,0:T(4,128)S(1)} %get-tuple-element.151, bf16[2,32,49,4,64]{2,1,0,4,3:T(8,128)(2,1)} %reshape.169), kind=kOutput, calls=%fused_computation.37 | convolution fusion | flops 80708096 | bytes 5720064 | tf_op jit(solution)/shard_map/fwhij,fwjhe->fwihe/dot_general | solution.py:38
  255.1 28.3 %gather_fusion.3 = bf16[3136,4,64]{2,1,0:T(4,128)(2,1)} fusion(bf16[2,1568,4,64]{3,2,1,0:T(4,128)(2,1)} %bitcast.91, s32[3136]{0:T(1024)S(1)} %reshape.162), kind=kCustom, calls=%fused_computation.3.clone | custom fusion | bytes 3236352 | tf_op jit(solution)/shard_map/jit(take_along_axis)/gather | solution.py:43
  311.2 124.0 %all-reduce.2.cloned.1.call-done = bf16[3136,1024]{1,0:T(8,128)(2,1)} async-done(((bf16[3136,1024]{1,0:T(8,128)(2,1)}), bf16[3136,1024]{1,0:T(8,128)(2,1)}) %all-reduce.2.cloned.1.call-update) | async-done | bytes 6422544 | tf_op jit(solution)/shard_map/psum | solution.py:72
  435.2 12.4 %bitcast_add_fusion.1 = f32[3136,1024]{1,0:T(8,128)} fusion(bf16[2,1568,1024]{2,1,0:T(8,128)(2,1)} %param.14, bf16[3136,1024]{1,0:T(8,128)(2,1)} %all-reduce.2.cloned.1.call-done), kind=kLoop, calls=%fused_computation.13 | loop fusion | flops 9633792 | bytes 25690112 | tf_op jit(solution)/shard_map/add | solution.py:72
  453.3 11.2 %convolution_bitcast_fusion = f32[3,3136,256]{2,1,0:T(8,128)} fusion(bf16[3,1024,256]{2,1,0:T(8,128)(2,1)S(1)} %copy-done.8, f32[3136,1024]{1,0:T(8,128)} %bitcast_add_fusion.1, f32[3136]{0:T(1024)S(1)} %add_rsqrt_fusion), kind=kOutput, calls=%fused_computation.20 | convolution fusion | flops 4938924032 | bytes 24064256 | tf_op jit(solution)/shard_map/td,kde->kte/dot_general | solution.py:74
  479.4 315.5 %while.29 = (s32[]{:T(128)}, f32[1568,256]{1,0:T(8,128)}, f32[256]{0:T(256)S(1)}, f32[1568,256]{1,0:T(8,128)S(1)}, s32[]{:T(128)}, /*index=5*/s32[]{:T(128)}) while((s32[]{:T(128)}, f32[1568,256]{1,0:T(8,128)}, f32[256]{0:T(256)S(1)}, f32[1568,256]{1,0:T(8,128)S(1)}, s32[]{:T(128)}, /*index=5*/s32[]{:T(128)}) %tuple.55), condition=%wide.region_9.11_spmd.clone, body=%wide.region_8.10_spmd.clone.sunk | while | flops 2007043 | bytes 9634935 | solution.py:111
  483.7 15.5 %collective-permute-done = bf16[1568,256]{1,0:T(8,128)(2,1)} collective-permute-done((bf16[1568,256]{1,0:T(8,128)(2,1)S(1)}, bf16[1568,256]{1,0:T(8,128)(2,1)}, u32[]{:S(2)}, u32[]{:S(2)}) %collective-permute-start) | collective-permute-done | bytes 802848 | tf_op jit(solution)/shard_map/while/body/eval_jaxpr/ppermute | solution.py:14
  508.5 14.6 %collective-permute-done = bf16[1568,256]{1,0:T(8,128)(2,1)} collective-permute-done((bf16[1568,256]{1,0:T(8,128)(2,1)S(1)}, bf16[1568,256]{1,0:T(8,128)(2,1)}, u32[]{:S(2)}, u32[]{:S(2)}) %collective-permute-start) | collective-permute-done | bytes 802848 | tf_op jit(solution)/shard_map/while/body/eval_jaxpr/ppermute | solution.py:14
  532.4 13.7 %collective-permute-done = bf16[1568,256]{1,0:T(8,128)(2,1)} collective-permute-done((bf16[1568,256]{1,0:T(8,128)(2,1)S(1)}, bf16[1568,256]{1,0:T(8,128)(2,1)}, u32[]{:S(2)}, u32[]{:S(2)}) %collective-permute-start) | collective-permute-done | bytes 802848 | tf_op jit(solution)/shard_map/while/body/eval_jaxpr/ppermute | solution.py:14
  555.3 12.8 %collective-permute-done = bf16[1568,256]{1,0:T(8,128)(2,1)} collective-permute-done((bf16[1568,256]{1,0:T(8,128)(2,1)S(1)}, bf16[1568,256]{1,0:T(8,128)(2,1)}, u32[]{:S(2)}, u32[]{:S(2)}) %collective-permute-start) | collective-permute-done | bytes 802848 | tf_op jit(solution)/shard_map/while/body/eval_jaxpr/ppermute | solution.py:14
  577.3 11.9 %collective-permute-done = bf16[1568,256]{1,0:T(8,128)(2,1)} collective-permute-done((bf16[1568,256]{1,0:T(8,128)(2,1)S(1)}, bf16[1568,256]{1,0:T(8,128)(2,1)}, u32[]{:S(2)}, u32[]{:S(2)}) %collective-permute-start) | collective-permute-done | bytes 802848 | tf_op jit(solution)/shard_map/while/body/eval_jaxpr/ppermute | solution.py:14
  599.0 10.9 %collective-permute-done = bf16[1568,256]{1,0:T(8,128)(2,1)} collective-permute-done((bf16[1568,256]{1,0:T(8,128)(2,1)S(1)}, bf16[1568,256]{1,0:T(8,128)(2,1)}, u32[]{:S(2)}, u32[]{:S(2)}) %collective-permute-start) | collective-permute-done | bytes 802848 | tf_op jit(solution)/shard_map/while/body/eval_jaxpr/ppermute | solution.py:14
  621.3 10.0 %collective-permute-done = bf16[1568,256]{1,0:T(8,128)(2,1)} collective-permute-done((bf16[1568,256]{1,0:T(8,128)(2,1)S(1)}, bf16[1568,256]{1,0:T(8,128)(2,1)}, u32[]{:S(2)}, u32[]{:S(2)}) %collective-permute-start) | collective-permute-done | bytes 802848 | tf_op jit(solution)/shard_map/while/body/eval_jaxpr/ppermute | solution.py:14
  760.8 9.5 %collective-permute-done = bf16[1568,256]{1,0:T(8,128)(2,1)} collective-permute-done((bf16[1568,256]{1,0:T(8,128)(2,1)S(1)}, bf16[1568,256]{1,0:T(8,128)(2,1)}, u32[]{:S(2)}, u32[]{:S(2)}) %collective-permute-start) | collective-permute-done | bytes 802848 | tf_op jit(solution)/shard_map/while/body/eval_jaxpr/ppermute | solution.py:14
  781.9 10.6 %collective-permute-done = bf16[1568,256]{1,0:T(8,128)(2,1)} collective-permute-done((bf16[1568,256]{1,0:T(8,128)(2,1)S(1)}, bf16[1568,256]{1,0:T(8,128)(2,1)}, u32[]{:S(2)}, u32[]{:S(2)}) %collective-permute-start) | collective-permute-done | bytes 802848 | tf_op jit(solution)/shard_map/while/body/eval_jaxpr/ppermute | solution.py:14
  803.7 91.7 %reduce-scatter.2.cloned.1.call-done = bf16[3136,256]{1,0:T(8,128)(2,1)} async-done(((bf16[3136,1024]{1,0:T(8,128)(2,1)}), bf16[3136,256]{1,0:T(8,128)(2,1)}) %reduce-scatter.2.cloned.1.call-update) | async-done | bytes 1605648 | tf_op jit(solution)/shard_map/reduce_scatter | solution.py:117
  (125 shorter events, 342.8 us)
Async XLA Ops:
  6.5 16.3 %copy-start = (bf16[3,1024,256]{2,1,0:T(8,128)(2,1)S(1)}, bf16[3,1024,256]{2,1,0:T(8,128)(2,1)}, u32[]{:S(2)}) copy-start(bf16[3,1024,256]{2,1,0:T(8,128)(2,1)} %param.17) | copy-start | bytes 4718596
  6.5 428.7 %all-reduce.2.cloned.1.call-start = ((), (), s32[]{:S(2)}) async-start(), calls=%async_computation.1 | async-start | bytes 12845056 | tf_op jit(solution)/shard_map/psum | solution.py:72
  173.3 15.7 %copy-start.3 = (bf16[2,1568,4,64]{1,0,3,2:T(2,128)(2,1)S(1)}, bf16[2,1568,4,64]{1,0,3,2:T(2,128)(2,1)}, u32[]{:S(2)}) copy-start(bf16[2,1568,4,64]{1,0,3,2:T(2,128)(2,1)} %get-tuple-element.146) | copy-start | bytes 4816900
  291.9 6.4 copy-start.4
  302.8 8.3 copy-start.6
  302.9 592.5 %reduce-scatter.2.cloned.1.call-start = ((), (), s32[]{:S(2)}) async-start(), calls=%async_computation.2 | async-start | bytes 8028160 | tf_op jit(solution)/shard_map/reduce_scatter | solution.py:117
  304.1 5.7 collective-permute-start.1
  447.6 5.7 copy-start.8
  479.7 19.6 %collective-permute-start = (bf16[1568,256]{1,0:T(8,128)(2,1)S(1)}, bf16[1568,256]{1,0:T(8,128)(2,1)}, u32[]{:S(2)}, u32[]{:S(2)}) collective-permute-start(bf16[1568,256]{1,0:T(8,128)(2,1)S(1)} %fusion.38), channel_id=1, source_target_pairs={{0,4},{4,8},{8,12},{12,16},{16,20},{20,24},{24,28},{28,32},{32,36}... | collective-permute-start | bytes 2408456 | tf_op jit(solution)/shard_map/while/body/eval_jaxpr/ppermute | solution.py:14
  503.4 19.8 %collective-permute-start = (bf16[1568,256]{1,0:T(8,128)(2,1)S(1)}, bf16[1568,256]{1,0:T(8,128)(2,1)}, u32[]{:S(2)}, u32[]{:S(2)}) collective-permute-start(bf16[1568,256]{1,0:T(8,128)(2,1)S(1)} %fusion.38), channel_id=1, source_target_pairs={{0,4},{4,8},{8,12},{12,16},{16,20},{20,24},{24,28},{28,32},{32,36}... | collective-permute-start | bytes 2408456 | tf_op jit(solution)/shard_map/while/body/eval_jaxpr/ppermute | solution.py:14
  527.2 18.9 %collective-permute-start = (bf16[1568,256]{1,0:T(8,128)(2,1)S(1)}, bf16[1568,256]{1,0:T(8,128)(2,1)}, u32[]{:S(2)}, u32[]{:S(2)}) collective-permute-start(bf16[1568,256]{1,0:T(8,128)(2,1)S(1)} %fusion.38), channel_id=1, source_target_pairs={{0,4},{4,8},{8,12},{12,16},{16,20},{20,24},{24,28},{28,32},{32,36}... | collective-permute-start | bytes 2408456 | tf_op jit(solution)/shard_map/while/body/eval_jaxpr/ppermute | solution.py:14
  550.2 18.0 %collective-permute-start = (bf16[1568,256]{1,0:T(8,128)(2,1)S(1)}, bf16[1568,256]{1,0:T(8,128)(2,1)}, u32[]{:S(2)}, u32[]{:S(2)}) collective-permute-start(bf16[1568,256]{1,0:T(8,128)(2,1)S(1)} %fusion.38), channel_id=1, source_target_pairs={{0,4},{4,8},{8,12},{12,16},{16,20},{20,24},{24,28},{28,32},{32,36}... | collective-permute-start | bytes 2408456 | tf_op jit(solution)/shard_map/while/body/eval_jaxpr/ppermute | solution.py:14
  572.2 17.0 %collective-permute-start = (bf16[1568,256]{1,0:T(8,128)(2,1)S(1)}, bf16[1568,256]{1,0:T(8,128)(2,1)}, u32[]{:S(2)}, u32[]{:S(2)}) collective-permute-start(bf16[1568,256]{1,0:T(8,128)(2,1)S(1)} %fusion.38), channel_id=1, source_target_pairs={{0,4},{4,8},{8,12},{12,16},{16,20},{20,24},{24,28},{28,32},{32,36}... | collective-permute-start | bytes 2408456 | tf_op jit(solution)/shard_map/while/body/eval_jaxpr/ppermute | solution.py:14
  593.3 16.7 %collective-permute-start = (bf16[1568,256]{1,0:T(8,128)(2,1)S(1)}, bf16[1568,256]{1,0:T(8,128)(2,1)}, u32[]{:S(2)}, u32[]{:S(2)}) collective-permute-start(bf16[1568,256]{1,0:T(8,128)(2,1)S(1)} %fusion.38), channel_id=1, source_target_pairs={{0,4},{4,8},{8,12},{12,16},{16,20},{20,24},{24,28},{28,32},{32,36}... | collective-permute-start | bytes 2408456 | tf_op jit(solution)/shard_map/while/body/eval_jaxpr/ppermute | solution.py:14
  614.0 17.3 %collective-permute-start = (bf16[1568,256]{1,0:T(8,128)(2,1)S(1)}, bf16[1568,256]{1,0:T(8,128)(2,1)}, u32[]{:S(2)}, u32[]{:S(2)}) collective-permute-start(bf16[1568,256]{1,0:T(8,128)(2,1)S(1)} %fusion.38), channel_id=1, source_target_pairs={{0,4},{4,8},{8,12},{12,16},{16,20},{20,24},{24,28},{28,32},{32,36}... | collective-permute-start | bytes 2408456 | tf_op jit(solution)/shard_map/while/body/eval_jaxpr/ppermute | solution.py:14
  635.4 16.4 %collective-permute-start = (bf16[1568,256]{1,0:T(8,128)(2,1)S(1)}, bf16[1568,256]{1,0:T(8,128)(2,1)}, u32[]{:S(2)}, u32[]{:S(2)}) collective-permute-start(bf16[1568,256]{1,0:T(8,128)(2,1)S(1)} %fusion.38), channel_id=1, source_target_pairs={{0,4},{4,8},{8,12},{12,16},{16,20},{20,24},{24,28},{28,32},{32,36}... | collective-permute-start | bytes 2408456 | tf_op jit(solution)/shard_map/while/body/eval_jaxpr/ppermute | solution.py:14
  655.8 15.4 %collective-permute-start = (bf16[1568,256]{1,0:T(8,128)(2,1)S(1)}, bf16[1568,256]{1,0:T(8,128)(2,1)}, u32[]{:S(2)}, u32[]{:S(2)}) collective-permute-start(bf16[1568,256]{1,0:T(8,128)(2,1)S(1)} %fusion.38), channel_id=1, source_target_pairs={{0,4},{4,8},{8,12},{12,16},{16,20},{20,24},{24,28},{28,32},{32,36}... | collective-permute-start | bytes 2408456 | tf_op jit(solution)/shard_map/while/body/eval_jaxpr/ppermute | solution.py:14
  675.3 15.4 %collective-permute-start = (bf16[1568,256]{1,0:T(8,128)(2,1)S(1)}, bf16[1568,256]{1,0:T(8,128)(2,1)}, u32[]{:S(2)}, u32[]{:S(2)}) collective-permute-start(bf16[1568,256]{1,0:T(8,128)(2,1)S(1)} %fusion.38), channel_id=1, source_target_pairs={{0,4},{4,8},{8,12},{12,16},{16,20},{20,24},{24,28},{28,32},{32,36}... | collective-permute-start | bytes 2408456 | tf_op jit(solution)/shard_map/while/body/eval_jaxpr/ppermute | solution.py:14
  694.8 15.4 %collective-permute-start = (bf16[1568,256]{1,0:T(8,128)(2,1)S(1)}, bf16[1568,256]{1,0:T(8,128)(2,1)}, u32[]{:S(2)}, u32[]{:S(2)}) collective-permute-start(bf16[1568,256]{1,0:T(8,128)(2,1)S(1)} %fusion.38), channel_id=1, source_target_pairs={{0,4},{4,8},{8,12},{12,16},{16,20},{20,24},{24,28},{28,32},{32,36}... | collective-permute-start | bytes 2408456 | tf_op jit(solution)/shard_map/while/body/eval_jaxpr/ppermute | solution.py:14
  714.3 15.4 %collective-permute-start = (bf16[1568,256]{1,0:T(8,128)(2,1)S(1)}, bf16[1568,256]{1,0:T(8,128)(2,1)}, u32[]{:S(2)}, u32[]{:S(2)}) collective-permute-start(bf16[1568,256]{1,0:T(8,128)(2,1)S(1)} %fusion.38), channel_id=1, source_target_pairs={{0,4},{4,8},{8,12},{12,16},{16,20},{20,24},{24,28},{28,32},{32,36}... | collective-permute-start | bytes 2408456 | tf_op jit(solution)/shard_map/while/body/eval_jaxpr/ppermute | solution.py:14
  733.8 15.7 %collective-permute-start = (bf16[1568,256]{1,0:T(8,128)(2,1)S(1)}, bf16[1568,256]{1,0:T(8,128)(2,1)}, u32[]{:S(2)}, u32[]{:S(2)}) collective-permute-start(bf16[1568,256]{1,0:T(8,128)(2,1)S(1)} %fusion.38), channel_id=1, source_target_pairs={{0,4},{4,8},{8,12},{12,16},{16,20},{20,24},{24,28},{28,32},{32,36}... | collective-permute-start | bytes 2408456 | tf_op jit(solution)/shard_map/while/body/eval_jaxpr/ppermute | solution.py:14
  753.5 16.8 %collective-permute-start = (bf16[1568,256]{1,0:T(8,128)(2,1)S(1)}, bf16[1568,256]{1,0:T(8,128)(2,1)}, u32[]{:S(2)}, u32[]{:S(2)}) collective-permute-start(bf16[1568,256]{1,0:T(8,128)(2,1)S(1)} %fusion.38), channel_id=1, source_target_pairs={{0,4},{4,8},{8,12},{12,16},{16,20},{20,24},{24,28},{28,32},{32,36}... | collective-permute-start | bytes 2408456 | tf_op jit(solution)/shard_map/while/body/eval_jaxpr/ppermute | solution.py:14
  774.4 18.1 %collective-permute-start = (bf16[1568,256]{1,0:T(8,128)(2,1)S(1)}, bf16[1568,256]{1,0:T(8,128)(2,1)}, u32[]{:S(2)}, u32[]{:S(2)}) collective-permute-start(bf16[1568,256]{1,0:T(8,128)(2,1)S(1)} %fusion.38), channel_id=1, source_target_pairs={{0,4},{4,8},{8,12},{12,16},{16,20},{20,24},{24,28},{28,32},{32,36}... | collective-permute-start | bytes 2408456 | tf_op jit(solution)/shard_map/while/body/eval_jaxpr/ppermute | solution.py:14
  803.7 95.7 %copy-start.1 = (bf16[3,1024,256]{2,1,0:T(8,128)(2,1)S(1)}, bf16[3,1024,256]{2,1,0:T(8,128)(2,1)}, u32[]{:S(2)}) copy-start(bf16[3,1024,256]{2,1,0:T(8,128)(2,1)} %param.17) | copy-start | bytes 4718596
  (3 other events, 10.4 us)
Sparse Core Ops, SparseCore 0:
  303.0 132.1 all-reduce.1
  803.8 91.5 reduce-scatter.1
where the time goes:
time: 916 us; the launch traced here: 907 us
  waiting for transfers between devices  375 us (41%)
  local copies, waits for them, and re-layouts  227 us (25%)
  other arithmetic  132 us (14%)
  starting transfers between devices  101 us (11%)
  matrix products  54.5 us (6%)
  between operations  16.5 us (2%)
    ppermute x16, waiting for transfers between devices, from_behind(): lax.ppermute(value, axis, [(source, source + steps) for source in range(l...  160 us
    psum x1, waiting for transfers between devices, per_device(): lax.psum(partial_mix.astype(jnp.bfloat16), 'head').astype(jnp.float32)  124 us
    gather x7, local copies, waits for them, and re-layouts, arrange(): reordered = jnp.take_along_axis(tensor, order_index, axis=1)  121 us
    ppermute x16, starting transfers between devices, from_behind(): lax.ppermute(value, axis, [(source, source + steps) for source in range(l...  101 us
    reduce_scatter x1, waiting for transfers between devices, per_device(): lax.psum_scatter(partial_out.astype(jnp.bfloat16), 'head', scatter_dimens...  91.7 us
    reshape x3, local copies, waits for them, and re-layouts, arrange(): reordered.reshape(frame_count, positions // WINDOW, WINDOW, number_of_hea...  44.4 us
    gather x3, local copies, waits for them, and re-layouts, window_attention(): return jnp.take_along_axis(blended, inverse[:, :, None, None], axis=1)  36.8 us
    convert_element_type x15, other arithmetic, relay_step(): from_behind(outgoing.astype(jnp.bfloat16), 'tm', 1).astype(outgoing.dtype)  36.2 us
  transfers between devices with their start and end apart: 18, of which 17 were waited for; matrix products, arithmetic and copies ran while one was open for 0% of the time, Pallas kernels for 0%

commit v1 on v0

--- a/solution.py
+++ b/solution.py
@@ -69,7 +69,9 @@
     )
     partial_mix = jnp.dot(attended, attend_out, preferred_element_type=jnp.float32)
     offset = lax.axis_index("head") * local_width
-    residual = inputs + lax.psum(partial_mix.astype(jnp.bfloat16), "head").astype(jnp.float32)
+    residual = inputs + jnp.sum(
+        lax.all_gather(partial_mix.astype(jnp.bfloat16), "head"), axis=0
+    ).astype(jnp.float32)
     normed_again = normalize(residual).astype(jnp.bfloat16)
     recur_proj = jnp.einsum(
         "td,kde->kte", normed_again, recur_weight, preferred_element_type=jnp.float32

time: 916 us -> 1040 us (1.14)
  waiting for transfers between devices: 375 us -> 475 us
  other arithmetic: 132 us -> 155 us
    all_gather x0 -> x1, waiting for transfers between devices: none -> 223 us  [per_device(): lax.all_gather(partial_mix.astype(jnp.bfloat16), 'head')]
    psum x1 -> x0, waiting for transfers between devices: 124 us -> none  [per_device(): lax.psum(partial_mix.astype(jnp.bfloat16), 'head').astype(jnp.float32)]
    reduce_sum x0 -> x1, other arithmetic: none -> 21.4 us  [per_device(): jnp.sum(lax.all_gather(partial_mix.astype(jnp.bfloat16), 'head'), axis=0)]
where the time goes in v1:
time: 1040 us; the launch traced here: 1030 us
  waiting for transfers between devices  475 us (46%)
  local copies, waits for them, and re-layouts  227 us (22%)
  other arithmetic  155 us (15%)
  starting transfers between devices  101 us (10%)
  matrix products  54.7 us (5%)
  between operations  16.5 us (2%)
    all_gather x1, waiting for transfers between devices, per_device(): lax.all_gather(partial_mix.astype(jnp.bfloat16), 'head')  223 us
    ppermute x16, waiting for transfers between devices, from_behind(): lax.ppermute(value, axis, [(source, source + steps) for source in range(l...  160 us
    gather x7, local copies, waits for them, and re-layouts, arrange(): reordered = jnp.take_along_axis(tensor, order_index, axis=1)  121 us
    ppermute x16, starting transfers between devices, from_behind(): lax.ppermute(value, axis, [(source, source + steps) for source in range(l...  101 us
    reduce_scatter x1, waiting for transfers between devices, per_device(): lax.psum_scatter(partial_out.astype(jnp.bfloat16), 'head', scatter_dimens...  92.4 us
    reshape x3, local copies, waits for them, and re-layouts, arrange(): reordered.reshape(frame_count, positions // WINDOW, WINDOW, number_of_hea...  44.4 us
    gather x3, local copies, waits for them, and re-layouts, window_attention(): return jnp.take_along_axis(blended, inverse[:, :, None, None], axis=1)  36.9 us
    convert_element_type x15, other arithmetic, relay_step(): from_behind(outgoing.astype(jnp.bfloat16), 'tm', 1).astype(outgoing.dtype)  36.2 us
  transfers between devices with their start and end apart: 18, of which 17 were waited for; matrix products, arithmetic and copies ran while one was open for 0% of the time, Pallas kernels for 0%

profile of v1, /device:TPU:1, one launch (start us, length us, event | category | flops | bytes accessed | tf_op | source)
XLA Modules:
  0.0 1029.8 jit_solution(10926681339691768028)
XLA Ops:
  33.3 28.2 %gather_fusion = bf16[3136,4,64]{2,1,0:T(4,128)(2,1)} fusion(bf16[2,1568,4,64]{3,2,1,0:T(4,128)(2,1)} %reshape.182, s32[3136]{0:T(1024)S(1)} %reshape.161), kind=kCustom, calls=%fused_computation.clone | custom fusion | bytes 3236352 | tf_op jit(solution)/shard_map/jit(take_along_axis)/gather | solution.py:26
  75.9 37.3 %gather_fusion.1 = bf16[3136,4,64]{2,1,0:T(4,128)(2,1)} fusion(bf16[2,1568,4,64]{3,2,1,0:T(4,128)(2,1)} %reshape.184, s32[3136]{0:T(1024)S(1)} %reshape.161), kind=kCustom, calls=%fused_computation.1.clone | custom fusion | bytes 3236352 | tf_op jit(solution)/shard_map/jit(take_along_axis)/gather | solution.py:26
  128.5 28.5 %gather_fusion.2 = bf16[3136,4,64]{2,1,0:T(4,128)(2,1)} fusion(bf16[2,1568,4,64]{3,2,1,0:T(4,128)(2,1)} %reshape.186, s32[3136]{0:T(1024)S(1)} %reshape.161), kind=kCustom, calls=%fused_computation.2.clone | custom fusion | bytes 3236352 | tf_op jit(solution)/shard_map/jit(take_along_axis)/gather | solution.py:26
  173.3 15.7 %reshape.185 = bf16[2,32,49,4,64]{2,1,0,4,3:T(8,128)(2,1)} reshape(bf16[2,1568,4,64]{1,0,3,2:T(2,128)(2,1)} %get-tuple-element.145) | data formatting | bytes 3211264 | tf_op jit(solution)/shard_map/reshape | solution.py:27
  189.0 14.4 %reshape.187 = bf16[2,32,49,4,64]{2,1,0,4,3:T(8,128)(2,1)} reshape(bf16[2,1568,4,64]{1,0,3,2:T(2,128)(2,1)S(1)} %copy-done.3) | data formatting | bytes 3211264 | tf_op jit(solution)/shard_map/reshape | solution.py:27
  203.4 15.2 %fusion.17 = f32[2,32,4,49,49]{3,4,2,1,0:T(8,128)S(1)} fusion(bf16[2,32,49,4,64]{2,1,0,4,3:T(8,128)(2,1)} %reshape.187, bf16[2,32,49,4,64]{2,1,0,4,3:T(8,128)(2,1)} %reshape.185), kind=kOutput, calls=%fused_computation.34 | convolution fusion | flops 78675968 | bytes 5669888 | tf_op jit(solution)/shard_map/fwihe,fwjhe->fwhij/dot_general | solution.py:31
  224.1 14.4 %reshape.183 = bf16[2,32,49,4,64]{2,1,0,4,3:T(8,128)(2,1)} reshape(bf16[2,1568,4,64]{1,0,3,2:T(2,128)(2,1)S(1)} %copy-done.2) | data formatting | bytes 3211264 | tf_op jit(solution)/shard_map/reshape | solution.py:27
  238.5 13.6 %convert_bitcast_fusion = bf16[2,32,49,4,64]{4,2,3,1,0:T(8,128)(2,1)S(1)} fusion(f32[2,32,4,49,49]{3,4,2,1,0:T(8,128)} %get-tuple-element.152, f32[2,32,4,49]{3,2,1,0:T(4,128)S(1)} %get-tuple-element.151, bf16[2,32,49,4,64]{2,1,0,4,3:T(8,128)(2,1)} %reshape.183), kind=kOutput, calls=%fused_computation.39 | convolution fusion | flops 80708096 | bytes 5720064 | tf_op jit(solution)/shard_map/fwhij,fwjhe->fwihe/dot_general | solution.py:38
  255.1 28.3 %gather_fusion.3 = bf16[3136,4,64]{2,1,0:T(4,128)(2,1)} fusion(bf16[2,1568,4,64]{3,2,1,0:T(4,128)(2,1)} %bitcast.96, s32[3136]{0:T(1024)S(1)} %reshape.176), kind=kCustom, calls=%fused_computation.3.clone | custom fusion | bytes 3236352 | tf_op jit(solution)/shard_map/jit(take_along_axis)/gather | solution.py:43
  311.2 223.2 %all-gather.3.cloned.1.call-done = bf16[12544,1024]{1,0:T(8,128)(2,1)} async-done(((bf16[3136,1024]{1,0:T(8,128)(2,1)}), bf16[12544,1024]{1,0:T(8,128)(2,1)}) %all-gather.3.cloned.1.call-update) | async-done | bytes 25690128 | tf_op jit(solution)/shard_map/all_gather | solution.py:73
  534.4 21.4 %reduce_sum.41 = bf16[3136,1024]{1,0:T(8,128)(2,1)} reduce(bf16[4,3136,1024]{2,1,0:T(8,128)(2,1)} %bitcast.88, bf16[]{:T(256)} %constant.34.clone.1), dimensions={0}, to_apply=%region_4.0 | reduce | flops 9633792 | bytes 32112642 | tf_op jit(solution)/shard_map/reduce_sum | solution.py:72
  555.9 12.4 %bitcast_add_fusion.1 = f32[3136,1024]{1,0:T(8,128)} fusion(bf16[2,1568,1024]{2,1,0:T(8,128)(2,1)} %param.14, bf16[3136,1024]{1,0:T(8,128)(2,1)} %reduce_sum.41), kind=kLoop, calls=%fused_computation.13 | loop fusion | flops 9633792 | bytes 25690112 | tf_op jit(solution)/shard_map/add | solution.py:72
  575.2 11.4 %convolution_bitcast_fusion = f32[3,3136,256]{2,1,0:T(8,128)} fusion(bf16[3,1024,256]{2,1,0:T(8,128)(2,1)} %param.19, f32[3136,1024]{1,0:T(8,128)} %bitcast_add_fusion.1, f32[3136]{0:T(1024)S(1)} %rsqrt.25), kind=kOutput, calls=%fused_computation.22 | convolution fusion | flops 4938924032 | bytes 24064256 | tf_op jit(solution)/shard_map/td,kde->kte/dot_general | solution.py:76
  601.4 316.0 %while.29 = (s32[]{:T(128)}, f32[1568,256]{1,0:T(8,128)}, f32[256]{0:T(256)S(1)}, f32[1568,256]{1,0:T(8,128)S(1)}, s32[]{:T(128)}, /*index=5*/s32[]{:T(128)}) while((s32[]{:T(128)}, f32[1568,256]{1,0:T(8,128)}, f32[256]{0:T(256)S(1)}, f32[1568,256]{1,0:T(8,128)S(1)}, s32[]{:T(128)}, /*index=5*/s32[]{:T(128)}) %tuple.55), condition=%wide.region_9.11_spmd.clone, body=%wide.region_8.10_spmd.clone.sunk | while | flops 2007043 | bytes 9634935 | solution.py:113
  606.0 15.6 %collective-permute-done = bf16[1568,256]{1,0:T(8,128)(2,1)} collective-permute-done((bf16[1568,256]{1,0:T(8,128)(2,1)S(1)}, bf16[1568,256]{1,0:T(8,128)(2,1)}, u32[]{:S(2)}, u32[]{:S(2)}) %collective-permute-start) | collective-permute-done | bytes 802848 | tf_op jit(solution)/shard_map/while/body/eval_jaxpr/ppermute | solution.py:14
  630.8 14.7 %collective-permute-done = bf16[1568,256]{1,0:T(8,128)(2,1)} collective-permute-done((bf16[1568,256]{1,0:T(8,128)(2,1)S(1)}, bf16[1568,256]{1,0:T(8,128)(2,1)}, u32[]{:S(2)}, u32[]{:S(2)}) %collective-permute-start) | collective-permute-done | bytes 802848 | tf_op jit(solution)/shard_map/while/body/eval_jaxpr/ppermute | solution.py:14
  654.7 13.7 %collective-permute-done = bf16[1568,256]{1,0:T(8,128)(2,1)} collective-permute-done((bf16[1568,256]{1,0:T(8,128)(2,1)S(1)}, bf16[1568,256]{1,0:T(8,128)(2,1)}, u32[]{:S(2)}, u32[]{:S(2)}) %collective-permute-start) | collective-permute-done | bytes 802848 | tf_op jit(solution)/shard_map/while/body/eval_jaxpr/ppermute | solution.py:14
  677.7 12.8 %collective-permute-done = bf16[1568,256]{1,0:T(8,128)(2,1)} collective-permute-done((bf16[1568,256]{1,0:T(8,128)(2,1)S(1)}, bf16[1568,256]{1,0:T(8,128)(2,1)}, u32[]{:S(2)}, u32[]{:S(2)}) %collective-permute-start) | collective-permute-done | bytes 802848 | tf_op jit(solution)/shard_map/while/body/eval_jaxpr/ppermute | solution.py:14
  699.7 11.9 %collective-permute-done = bf16[1568,256]{1,0:T(8,128)(2,1)} collective-permute-done((bf16[1568,256]{1,0:T(8,128)(2,1)S(1)}, bf16[1568,256]{1,0:T(8,128)(2,1)}, u32[]{:S(2)}, u32[]{:S(2)}) %collective-permute-start) | collective-permute-done | bytes 802848 | tf_op jit(solution)/shard_map/while/body/eval_jaxpr/ppermute | solution.py:14
  721.5 11.0 %collective-permute-done = bf16[1568,256]{1,0:T(8,128)(2,1)} collective-permute-done((bf16[1568,256]{1,0:T(8,128)(2,1)S(1)}, bf16[1568,256]{1,0:T(8,128)(2,1)}, u32[]{:S(2)}, u32[]{:S(2)}) %collective-permute-start) | collective-permute-done | bytes 802848 | tf_op jit(solution)/shard_map/while/body/eval_jaxpr/ppermute | solution.py:14
  743.9 10.1 collective-permute-done
  883.4 9.4 collective-permute-done
  904.5 10.5 %collective-permute-done = bf16[1568,256]{1,0:T(8,128)(2,1)} collective-permute-done((bf16[1568,256]{1,0:T(8,128)(2,1)S(1)}, bf16[1568,256]{1,0:T(8,128)(2,1)}, u32[]{:S(2)}, u32[]{:S(2)}) %collective-permute-start) | collective-permute-done | bytes 802848 | tf_op jit(solution)/shard_map/while/body/eval_jaxpr/ppermute | solution.py:14
  926.2 92.4 %reduce-scatter.2.cloned.1.call-done = bf16[3136,256]{1,0:T(8,128)(2,1)} async-done(((bf16[3136,1024]{1,0:T(8,128)(2,1)}), bf16[3136,256]{1,0:T(8,128)(2,1)}) %reduce-scatter.2.cloned.1.call-update) | async-done | bytes 1605648 | tf_op jit(solution)/shard_map/reduce_scatter | solution.py:119
  (125 shorter events, 353.5 us)
Async XLA Ops:
  6.5 16.3 %copy-start = (bf16[3,1024,256]{2,1,0:T(8,128)(2,1)S(1)}, bf16[3,1024,256]{2,1,0:T(8,128)(2,1)}, u32[]{:S(2)}) copy-start(bf16[3,1024,256]{2,1,0:T(8,128)(2,1)} %param.17) | copy-start | bytes 4718596
  6.5 527.9 %all-gather.3.cloned.1.call-start = ((), (), s32[]{:S(2)}) async-start(), calls=%async_computation.2 | async-start | bytes 32112640 | tf_op jit(solution)/shard_map/all_gather | solution.py:73
  173.3 15.7 %copy-start.3 = (bf16[2,1568,4,64]{1,0,3,2:T(2,128)(2,1)S(1)}, bf16[2,1568,4,64]{1,0,3,2:T(2,128)(2,1)}, u32[]{:S(2)}) copy-start(bf16[2,1568,4,64]{1,0,3,2:T(2,128)(2,1)} %get-tuple-element.146) | copy-start | bytes 4816900
  218.6 5.5 copy-start.2
  291.9 6.4 copy-start.4
  302.9 8.2 copy-start.6
  302.9 715.6 %reduce-scatter.2.cloned.1.call-start = ((), (), s32[]{:S(2)}) async-start(), calls=%async_computation.1 | async-start | bytes 8028160 | tf_op jit(solution)/shard_map/reduce_scatter | solution.py:119
  304.1 5.7 collective-permute-start.1
  601.9 19.6 %collective-permute-start = (bf16[1568,256]{1,0:T(8,128)(2,1)S(1)}, bf16[1568,256]{1,0:T(8,128)(2,1)}, u32[]{:S(2)}, u32[]{:S(2)}) collective-permute-start(bf16[1568,256]{1,0:T(8,128)(2,1)S(1)} %fusion.40), channel_id=1, source_target_pairs={{0,4},{4,8},{8,12},{12,16},{16,20},{20,24},{24,28},{28,32},{32,36}... | collective-permute-start | bytes 2408456 | tf_op jit(solution)/shard_map/while/body/eval_jaxpr/ppermute | solution.py:14
  625.6 19.8 %collective-permute-start = (bf16[1568,256]{1,0:T(8,128)(2,1)S(1)}, bf16[1568,256]{1,0:T(8,128)(2,1)}, u32[]{:S(2)}, u32[]{:S(2)}) collective-permute-start(bf16[1568,256]{1,0:T(8,128)(2,1)S(1)} %fusion.40), channel_id=1, source_target_pairs={{0,4},{4,8},{8,12},{12,16},{16,20},{20,24},{24,28},{28,32},{32,36}... | collective-permute-start | bytes 2408456 | tf_op jit(solution)/shard_map/while/body/eval_jaxpr/ppermute | solution.py:14
  649.5 18.9 %collective-permute-start = (bf16[1568,256]{1,0:T(8,128)(2,1)S(1)}, bf16[1568,256]{1,0:T(8,128)(2,1)}, u32[]{:S(2)}, u32[]{:S(2)}) collective-permute-start(bf16[1568,256]{1,0:T(8,128)(2,1)S(1)} %fusion.40), channel_id=1, source_target_pairs={{0,4},{4,8},{8,12},{12,16},{16,20},{20,24},{24,28},{28,32},{32,36}... | collective-permute-start | bytes 2408456 | tf_op jit(solution)/shard_map/while/body/eval_jaxpr/ppermute | solution.py:14
  672.5 18.0 %collective-permute-start = (bf16[1568,256]{1,0:T(8,128)(2,1)S(1)}, bf16[1568,256]{1,0:T(8,128)(2,1)}, u32[]{:S(2)}, u32[]{:S(2)}) collective-permute-start(bf16[1568,256]{1,0:T(8,128)(2,1)S(1)} %fusion.40), channel_id=1, source_target_pairs={{0,4},{4,8},{8,12},{12,16},{16,20},{20,24},{24,28},{28,32},{32,36}... | collective-permute-start | bytes 2408456 | tf_op jit(solution)/shard_map/while/body/eval_jaxpr/ppermute | solution.py:14
  694.6 17.1 %collective-permute-start = (bf16[1568,256]{1,0:T(8,128)(2,1)S(1)}, bf16[1568,256]{1,0:T(8,128)(2,1)}, u32[]{:S(2)}, u32[]{:S(2)}) collective-permute-start(bf16[1568,256]{1,0:T(8,128)(2,1)S(1)} %fusion.40), channel_id=1, source_target_pairs={{0,4},{4,8},{8,12},{12,16},{16,20},{20,24},{24,28},{28,32},{32,36}... | collective-permute-start | bytes 2408456 | tf_op jit(solution)/shard_map/while/body/eval_jaxpr/ppermute | solution.py:14
  715.7 16.8 %collective-permute-start = (bf16[1568,256]{1,0:T(8,128)(2,1)S(1)}, bf16[1568,256]{1,0:T(8,128)(2,1)}, u32[]{:S(2)}, u32[]{:S(2)}) collective-permute-start(bf16[1568,256]{1,0:T(8,128)(2,1)S(1)} %fusion.40), channel_id=1, source_target_pairs={{0,4},{4,8},{8,12},{12,16},{16,20},{20,24},{24,28},{28,32},{32,36}... | collective-permute-start | bytes 2408456 | tf_op jit(solution)/shard_map/while/body/eval_jaxpr/ppermute | solution.py:14
  736.6 17.3 %collective-permute-start = (bf16[1568,256]{1,0:T(8,128)(2,1)S(1)}, bf16[1568,256]{1,0:T(8,128)(2,1)}, u32[]{:S(2)}, u32[]{:S(2)}) collective-permute-start(bf16[1568,256]{1,0:T(8,128)(2,1)S(1)} %fusion.40), channel_id=1, source_target_pairs={{0,4},{4,8},{8,12},{12,16},{16,20},{20,24},{24,28},{28,32},{32,36}... | collective-permute-start | bytes 2408456 | tf_op jit(solution)/shard_map/while/body/eval_jaxpr/ppermute | solution.py:14
  758.0 16.4 %collective-permute-start = (bf16[1568,256]{1,0:T(8,128)(2,1)S(1)}, bf16[1568,256]{1,0:T(8,128)(2,1)}, u32[]{:S(2)}, u32[]{:S(2)}) collective-permute-start(bf16[1568,256]{1,0:T(8,128)(2,1)S(1)} %fusion.40), channel_id=1, source_target_pairs={{0,4},{4,8},{8,12},{12,16},{16,20},{20,24},{24,28},{28,32},{32,36}... | collective-permute-start | bytes 2408456 | tf_op jit(solution)/shard_map/while/body/eval_jaxpr/ppermute | solution.py:14
  778.5 15.4 %collective-permute-start = (bf16[1568,256]{1,0:T(8,128)(2,1)S(1)}, bf16[1568,256]{1,0:T(8,128)(2,1)}, u32[]{:S(2)}, u32[]{:S(2)}) collective-permute-start(bf16[1568,256]{1,0:T(8,128)(2,1)S(1)} %fusion.40), channel_id=1, source_target_pairs={{0,4},{4,8},{8,12},{12,16},{16,20},{20,24},{24,28},{28,32},{32,36}... | collective-permute-start | bytes 2408456 | tf_op jit(solution)/shard_map/while/body/eval_jaxpr/ppermute | solution.py:14
  797.9 15.4 %collective-permute-start = (bf16[1568,256]{1,0:T(8,128)(2,1)S(1)}, bf16[1568,256]{1,0:T(8,128)(2,1)}, u32[]{:S(2)}, u32[]{:S(2)}) collective-permute-start(bf16[1568,256]{1,0:T(8,128)(2,1)S(1)} %fusion.40), channel_id=1, source_target_pairs={{0,4},{4,8},{8,12},{12,16},{16,20},{20,24},{24,28},{28,32},{32,36}... | collective-permute-start | bytes 2408456 | tf_op jit(solution)/shard_map/while/body/eval_jaxpr/ppermute | solution.py:14
  817.4 15.4 %collective-permute-start = (bf16[1568,256]{1,0:T(8,128)(2,1)S(1)}, bf16[1568,256]{1,0:T(8,128)(2,1)}, u32[]{:S(2)}, u32[]{:S(2)}) collective-permute-start(bf16[1568,256]{1,0:T(8,128)(2,1)S(1)} %fusion.40), channel_id=1, source_target_pairs={{0,4},{4,8},{8,12},{12,16},{16,20},{20,24},{24,28},{28,32},{32,36}... | collective-permute-start | bytes 2408456 | tf_op jit(solution)/shard_map/while/body/eval_jaxpr/ppermute | solution.py:14
  836.9 15.4 %collective-permute-start = (bf16[1568,256]{1,0:T(8,128)(2,1)S(1)}, bf16[1568,256]{1,0:T(8,128)(2,1)}, u32[]{:S(2)}, u32[]{:S(2)}) collective-permute-start(bf16[1568,256]{1,0:T(8,128)(2,1)S(1)} %fusion.40), channel_id=1, source_target_pairs={{0,4},{4,8},{8,12},{12,16},{16,20},{20,24},{24,28},{28,32},{32,36}... | collective-permute-start | bytes 2408456 | tf_op jit(solution)/shard_map/while/body/eval_jaxpr/ppermute | solution.py:14
  856.4 15.7 %collective-permute-start = (bf16[1568,256]{1,0:T(8,128)(2,1)S(1)}, bf16[1568,256]{1,0:T(8,128)(2,1)}, u32[]{:S(2)}, u32[]{:S(2)}) collective-permute-start(bf16[1568,256]{1,0:T(8,128)(2,1)S(1)} %fusion.40), channel_id=1, source_target_pairs={{0,4},{4,8},{8,12},{12,16},{16,20},{20,24},{24,28},{28,32},{32,36}... | collective-permute-start | bytes 2408456 | tf_op jit(solution)/shard_map/while/body/eval_jaxpr/ppermute | solution.py:14
  876.2 16.7 %collective-permute-start = (bf16[1568,256]{1,0:T(8,128)(2,1)S(1)}, bf16[1568,256]{1,0:T(8,128)(2,1)}, u32[]{:S(2)}, u32[]{:S(2)}) collective-permute-start(bf16[1568,256]{1,0:T(8,128)(2,1)S(1)} %fusion.40), channel_id=1, source_target_pairs={{0,4},{4,8},{8,12},{12,16},{16,20},{20,24},{24,28},{28,32},{32,36}... | collective-permute-start | bytes 2408456 | tf_op jit(solution)/shard_map/while/body/eval_jaxpr/ppermute | solution.py:14
  896.9 18.1 %collective-permute-start = (bf16[1568,256]{1,0:T(8,128)(2,1)S(1)}, bf16[1568,256]{1,0:T(8,128)(2,1)}, u32[]{:S(2)}, u32[]{:S(2)}) collective-permute-start(bf16[1568,256]{1,0:T(8,128)(2,1)S(1)} %fusion.40), channel_id=1, source_target_pairs={{0,4},{4,8},{8,12},{12,16},{16,20},{20,24},{24,28},{28,32},{32,36}... | collective-permute-start | bytes 2408456 | tf_op jit(solution)/shard_map/while/body/eval_jaxpr/ppermute | solution.py:14
  926.2 96.3 %copy-start.1 = (bf16[3,1024,256]{2,1,0:T(8,128)(2,1)S(1)}, bf16[3,1024,256]{2,1,0:T(8,128)(2,1)}, u32[]{:S(2)}) copy-start(bf16[3,1024,256]{2,1,0:T(8,128)(2,1)} %param.17) | copy-start | bytes 4718596
  (2 other events, 4.9 us)
Sparse Core Ops, SparseCore 0:
  303.1 231.3 all-gather.2
  926.3 92.2 reduce-scatter.1
